TPU v7x, 32 devices: a whole 2x2x4 slice. The times are simulated.
32 devices in a mesh: ka: 16 (over z, y, core), freq: 2 (over x).
Axes of the slice: x: 2, y: 2, z: 4, core: 2. Of those that a mesh axis runs over, the one named last changes fastest.
Arguments:
- energy: float32 [16, 128], P('ka'), may hold values from -2.4 to 2.4, as said below
- projector: float32 [16, 2, 128, 40], P('ka'), may hold values from -0.25 to 0.25
- self_energy: float32 [32, 2, 40, 40], P('freq'), may hold values from -0.5 to 0.5
- multiplicity: int32 [16], P('ka'), may hold values from 1 to 5
- orbitals: float32 [16, 2, 128, 16, 256], P('ka', None, None, None, 'freq'), may hold values from -12 to 12
- owner: int32 [16], replicated, may hold values from 0 to 15, each once
- rotation: float32 [40, 40], replicated, may hold values from -1 to 1
Outputs:
- local_green: float32 [32, 2, 40, 40], P('freq')
- slab_charge: float32 [16, 256], P('ka', 'freq')
Inputs may be any that keep to these rules, and one draw needn't show every extreme that they name: Every band energy has a magnitude between 1.6 and 2.4. `owner`: each ka index owns exactly one slab.
All inputs are finite; a program needn't handle non-finite values.
Results may differ from a plain program's by a relative error of at most 0.0001.
Values sent between devices are 32-bit elements; how exact they have to be, the bound alone decides.
A program may use at most 64 MiB of HBM per device.

v0:
```python
import functools
import math

import jax
import jax.numpy as jnp
from jax import lax
from jax.experimental import pallas as pl
from jax.experimental.pallas import tpu as pltpu
from jax.sharding import PartitionSpec as P

NS_STEPS = 3
GROUP = 8
HALF = 64
F32 = jnp.float32
BF16 = jnp.bfloat16
MESH = pl.DeviceIdType.MESH


def split(value):
    high = value.astype(BF16)
    return high, (value - high.astype(F32)).astype(BF16)


def dot3(first, second):
    one = functools.partial(jnp.dot, preferred_element_type=F32)
    return one(first[0], second[0]) + (one(first[1], second[0]) + one(first[0], second[1]))


def exact_dot(first, second):
    return jnp.dot(first, second, precision=lax.Precision.HIGHEST, preferred_element_type=F32)


def lanes(shape):
    return lax.broadcasted_iota(jnp.int32, shape, len(shape) - 1)


def rows(shape):
    return lax.broadcasted_iota(jnp.int32, shape, 0)


def swap(pair):
    turned = pltpu.roll(pair, HALF, 1)
    return jnp.where(lanes(pair.shape) < HALF, -turned, turned)


def tall(top, bottom):
    gap = jnp.zeros((HALF - top.shape[0], top.shape[1]), F32)
    return jnp.concatenate([top, gap, bottom, gap], axis=0)


def packed(real, imag):
    gap = jnp.zeros((real.shape[0], HALF - real.shape[1]), F32)
    return jnp.concatenate([real, gap, imag, gap], axis=1)


def green_kernel(thermal, mult_ref, energy_ref, proj_ref, self_ref, density_ref, local_ref, total_ref):
    slots, orbs = self_ref.shape[0], self_ref.shape[2]
    bands = energy_ref.shape[1]
    freq_count, freq_at = lax.axis_size("freq"), lax.axis_index("freq")
    weight = mult_ref[0].astype(F32)
    pair = packed(proj_ref[0, 0], proj_ref[0, 1])
    swapped = swap(pair)
    across = jnp.transpose(pair)
    across_re, across_im = across[:orbs], across[HALF : HALF + orbs]
    weights_pp = split(jnp.concatenate([pair, swapped], axis=0))
    energy = energy_ref[...]
    energy_col = jnp.transpose(jnp.broadcast_to(energy, (bands, bands)))
    lane = lanes((orbs, 2 * HALF))
    unit = jnp.where(lane == rows((orbs, 2 * HALF)), 1.0, 0.0).astype(F32)
    total_ref[...] = jnp.zeros_like(total_ref)

    def body(step, carry):
        at = [step * GROUP + g for g in range(GROUP)]
        omega = [(2 * (q * freq_count + freq_at) + 1).astype(F32) * (math.pi * thermal) for q in at]
        inv = [1.0 / (w * w + energy * energy) for w in omega]
        bare_re = [-energy * v for v in inv]
        bare_im = [-w * v for w, v in zip(omega, inv)]
        c_re = [across_re * r + across_im * i for r, i in zip(bare_re, bare_im)]
        c_im = [across_re * i - across_im * r for r, i in zip(bare_re, bare_im)]
        g = [dot3(split(jnp.concatenate([a, b], axis=1)), weights_pp) for a, b in zip(c_re, c_im)]
        s = [split(packed(self_ref[q, 0], self_ref[q, 1])) for q in at]
        first = [
            split(tall(jnp.concatenate([a, b, c], axis=1), jnp.concatenate([-b, a, swap(c)], axis=1)))
            for a, b, c in zip(c_re, c_im, g)
        ]
        out = [dot3(a, b) for a, b in zip(s, first)]
        sc_re = [o[:, :bands] for o in out]
        sc_im = [o[:, bands : 2 * bands] for o in out]
        a1 = [o[:, 2 * bands :] for o in out]
        real_a = [split(tall(a, swap(a))) for a in a1]
        a2 = [dot3(split(a), r) for a, r in zip(a1, real_a)]
        a3 = [dot3(split(a), r) for a, r in zip(a2, real_a)]
        h = [a + b + c for a, b, c in zip(a1, a2, a3)]
        poly = [unit + a + dot3(split(a), split(tall(b, swap(b)))) for a, b in zip(h, a3)]
        real_sc = [
            split(tall(jnp.concatenate([a, b], axis=1), jnp.concatenate([-b, a], axis=1)))
            for a, b in zip(sc_re, sc_im)
        ]
        poly = [split(p) for p in poly]
        v = [dot3(p, r) for p, r in zip(poly, real_sc)]
        wg = [dot3(p, r) for p, r in zip(poly, real_a)]
        for q, one_g, one_w in zip(at, g, wg):
            one = weight * (one_g + dot3(split(one_g), split(tall(one_w, swap(one_w)))))
            local_ref[q] = jnp.where(lane >= HALF + orbs, weight, one)
        gain = None
        for w, one_v in zip(omega, v):
            inv_col = 1.0 / (w * w + energy_col * energy_col)
            left = split(pair * (-energy_col * inv_col) + swapped * (-w * inv_col))
            v_re, v_im = one_v[:, :bands], one_v[:, bands:]
            right = split(tall(one_v, jnp.concatenate([-v_im, v_re], axis=1)))
            term = dot3(left, right)
            gain = term if gain is None else gain + term
        total_ref[...] += gain
        return carry

    lax.fori_loop(0, slots // GROUP, body, 0)
    e_re, e_im = total_ref[:, :bands], total_ref[:, bands:]
    d_re = thermal * (e_re + jnp.transpose(e_re))
    d_im = thermal * (e_im - jnp.transpose(e_im))
    square = (bands, bands)
    density_ref[...] = jnp.where(rows(square) <= lanes(square), d_re, d_im)


def exchange_kernel(
    ka_count, freq_count, mult_ref, owner_ref, density_ref, local_ref, rotation_ref, orbital_ref,
    green_ref, slab_ref,
    columns, high, low, density_in, local_in, mine, gathered, rates, charge_out, charge_in,
    orbital_sem, density_sem, local_sem, gather_sem, charge_sem,
):
    me, freq_me = lax.axis_index("ka"), lax.axis_index("freq")
    slots, orbs, wide = local_ref.shape
    bands = density_ref.shape[0]
    slabs = columns.shape[0] // (2 * bands)
    owners = min(slots, ka_count)
    each = slots // owners

    load = pltpu.make_async_copy(orbital_ref, columns, orbital_sem)
    load.start()

    barrier = pltpu.get_barrier_semaphore()
    for j in range(1, ka_count):
        pl.semaphore_signal(barrier, inc=1, device_id={"ka": lax.rem(me + j, ka_count)}, device_id_type=MESH)
    for j in range(1, freq_count):
        pl.semaphore_signal(
            barrier, inc=1, device_id={"freq": lax.rem(freq_me + j, freq_count)}, device_id_type=MESH
        )
    pl.semaphore_wait(barrier, ka_count + freq_count - 2)

    density_copies = []
    for j in range(1, freq_count):
        density_copies.append(
            pltpu.make_async_remote_copy(
                src_ref=density_ref, dst_ref=density_in.at[j - 1],
                send_sem=density_sem.at[0, j - 1], recv_sem=density_sem.at[1, j - 1],
                device_id={"freq": lax.rem(freq_me + j, freq_count)}, device_id_type=MESH,
            )
        )
        density_copies[-1].start()

    def when_owner(index, action):
        if owners == ka_count:
            action()
        else:
            pl.when(index < owners)(action)

    def chunk(index):
        return pl.ds(index * each, each)

    local_copies = []
    for j in range(1, ka_count):
        to = lax.rem(me + j, ka_count)
        aim = to if owners == ka_count else jnp.minimum(to, owners - 1)
        copy = pltpu.make_async_remote_copy(
            src_ref=local_ref.at[chunk(aim)], dst_ref=local_in.at[j - 1],
            send_sem=local_sem.at[0, j - 1], recv_sem=local_sem.at[1, j - 1],
            device_id={"ka": to}, device_id_type=MESH,
        )
        local_copies.append((copy, to))
        when_owner(to, copy.start)

    load.wait()
    for s in range(slabs):
        one = columns[pl.ds(s, 2 * bands, stride=slabs), :]
        high[s], low[s] = split(one)

    gather_copies = []
    for j in range(1, ka_count):
        to = lax.rem(me + j, ka_count)
        place = me if owners == ka_count else jnp.minimum(me, owners - 1)
        gather_copies.append(
            pltpu.make_async_remote_copy(
                src_ref=mine, dst_ref=gathered.at[chunk(place)],
                send_sem=gather_sem.at[0, j - 1], recv_sem=gather_sem.at[1, j - 1],
                device_id={"ka": to}, device_id_type=MESH,
            )
        )

    def reduce_and_send():
        for copy, _ in local_copies:
            copy.wait_recv()
        turn = rotation_ref[...]
        gap = jnp.zeros((orbs, HALF - orbs), F32)
        zero = jnp.zeros((orbs, HALF), F32)
        right = tall(jnp.concatenate([turn, gap, zero], axis=1), jnp.concatenate([zero, turn, gap], axis=1))
        left = jnp.transpose(turn)
        for e in range(each):
            acc = local_ref[me * each + e]
            for j in range(1, ka_count):
                acc = acc + local_in[j - 1, e]
            share = acc / acc[:1, wide - 1 :]
            mine[e] = exact_dot(left, exact_dot(share, right))
        for copy in gather_copies:
            copy.start()

    when_owner(me, reduce_and_send)
    for copy, to in local_copies:
        when_owner(to, copy.wait_send)

    for copy in density_copies:
        copy.wait()
    density = density_ref[...]
    for j in range(1, freq_count):
        density = density + density_in[j - 1]
    square = (bands, bands)
    row, lane = rows(square), lanes(square)
    upper = jnp.where(row < lane, 2.0 * density, jnp.where(row == lane, density, 0.0))
    lower = jnp.where(row > lane, 2.0 * density, 0.0)
    cross = lower - jnp.transpose(lower)
    form = split(
        jnp.concatenate(
            [
                jnp.concatenate([upper, jnp.zeros(square, F32)], axis=1),
                jnp.concatenate([cross, upper], axis=1),
            ],
            axis=0,
        )
    )
    weight = mult_ref[0].astype(F32)
    for s in range(slabs):
        product = dot3(form, (high[s], low[s]))
        one = high[s].astype(F32) + low[s].astype(F32)
        rates[pl.ds(s, 1), :] = weight * jnp.sum(product * one, axis=0, keepdims=True)
    selector = jnp.where(owner_ref[...] == rows((slabs, slabs)), 1.0, 0.0).astype(F32)
    owned = exact_dot(selector, rates[...])
    for d in range(slabs):
        charge_out[d, 0:1, :] = owned[d : d + 1]
        charge_out[d, 1:2, :] = jnp.full((1, owned.shape[1]), weight, F32)
    charge_copies = []
    for j in range(1, ka_count):
        to = lax.rem(me + j, ka_count)
        copy = pltpu.make_async_remote_copy(
            src_ref=charge_out.at[to], dst_ref=charge_in.at[j - 1],
            send_sem=charge_sem.at[0, j - 1], recv_sem=charge_sem.at[1, j - 1],
            device_id={"ka": to}, device_id_type=MESH,
        )
        copy.start()
        charge_copies.append(copy)

    def store(q, value):
        green_ref[q, 0] = value[:, :orbs]
        green_ref[q, 1] = pltpu.roll(value, HALF, 1)[:, :orbs]

    def own_place():
        for e in range(each):
            store(me * each + e, mine[e])

    for j, copy in enumerate(gather_copies, 1):
        source = lax.rem(me + ka_count - j, ka_count)

        def take(copy=copy, source=source):
            copy.wait_recv()
            for e in range(each):
                store(source * each + e, gathered[source * each + e])

        when_owner(source, take)
    when_owner(me, own_place)

    def sent():
        for copy in gather_copies:
            copy.wait_send()

    when_owner(me, sent)
    for copy in charge_copies:
        copy.wait()
    acc = charge_out[me]
    for j in range(1, ka_count):
        acc = acc + charge_in[j - 1]
    slab_ref[...] = acc[0:1] / acc[1:2]


def local(energy, projector, self_energy, multiplicity, orbitals, owner, rotation):
    slots, orbs = self_energy.shape[0], self_energy.shape[2]
    bands = energy.shape[1]
    slab_count, point_count = orbitals.shape[3], orbitals.shape[4]
    freq_count, ka_count = lax.axis_size("freq"), lax.axis_size("ka")
    thermal = 0.25 / (slots * freq_count)
    vmem = pl.BlockSpec(memory_space=pltpu.VMEM)
    smem = pl.BlockSpec(memory_space=pltpu.SMEM)
    density, local_sum = pl.pallas_call(
        functools.partial(green_kernel, thermal),
        out_shape=(
            jax.ShapeDtypeStruct((bands, bands), F32),
            jax.ShapeDtypeStruct((slots, orbs, 2 * HALF), F32),
        ),
        in_specs=[smem, vmem, vmem, vmem],
        out_specs=(vmem, vmem),
        scratch_shapes=[pltpu.VMEM((bands, 2 * bands), F32)],
        name="green",
    )(multiplicity, energy, projector, self_energy)
    owners = min(slots, ka_count)
    each = slots // owners
    dma = pltpu.SemaphoreType.DMA
    columns = orbitals.reshape(2 * bands * slab_count, point_count)
    return pl.pallas_call(
        functools.partial(exchange_kernel, ka_count, freq_count),
        out_shape=(
            jax.ShapeDtypeStruct((slots, 2, orbs, orbs), F32),
            jax.ShapeDtypeStruct((1, point_count), F32),
        ),
        in_specs=[smem, vmem, vmem, vmem, vmem, pl.BlockSpec(memory_space=pl.ANY)],
        out_specs=(vmem, vmem),
        scratch_shapes=[
            pltpu.VMEM(columns.shape, F32),
            pltpu.VMEM((slab_count, 2 * bands, point_count), BF16),
            pltpu.VMEM((slab_count, 2 * bands, point_count), BF16),
            pltpu.VMEM((max(freq_count - 1, 1), bands, bands), F32),
            pltpu.VMEM((ka_count - 1, each, orbs, 2 * HALF), F32),
            pltpu.VMEM((each, orbs, 2 * HALF), F32),
            pltpu.VMEM((slots, orbs, 2 * HALF), F32),
            pltpu.VMEM((slab_count, point_count), F32),
            pltpu.VMEM((slab_count, 2, point_count), F32),
            pltpu.VMEM((ka_count - 1, 2, point_count), F32),
            dma,
            dma((2, max(freq_count - 1, 1))),
            dma((2, ka_count - 1)),
            dma((2, ka_count - 1)),
            dma((2, ka_count - 1)),
        ],
        compiler_params=pltpu.CompilerParams(collective_id=0, has_side_effects=True),
        name="exchange",
    )(multiplicity, owner.reshape(1, slab_count), density, local_sum, rotation, columns)


def solution(mesh):
    in_specs = (
        P("ka", None),
        P("ka", None, None, None),
        P("freq", None, None, None),
        P("ka"),
        P("ka", None, None, None, "freq"),
        P(),
        P(),
    )
    out_specs = (P("freq", None, None, None), P("ka", "freq"))
    return jax.shard_map(local, mesh=mesh, in_specs=in_specs, out_specs=out_specs, check_vma=False)
```

profile of v0, /device:TPU:0, one launch (start us, length us, event | category | flops | bytes accessed | tf_op | source)
XLA Modules:
  0.0 40.2 jit_solution(17380264120540671117)
XLA Ops:
  1.3 1.5 %copy.9.proj_ref = f32[1,2,128,40]{3,2,1,0:T(8,128)} copy(f32[1,2,128,40]{2,3,1,0:T(8,128)} %param.8) | data formatting | bytes 81920 | tf_op args[1]
  2.8 7.0 %green.1 = (f32[128,128]{1,0:T(8,128)}, f32[16,40,128]{2,1,0:T(8,128)}) custom-call(s32[1]{0:T(128)S(6)} %copy.12.mult_ref, f32[1,128]{1,0:T(1,128)} %energy_ref.1, f32[1,2,128,40]{3,2,1,0:T(8,128)} %copy.9.proj_ref, f32[16,2,40,40]{3,2,1,0:T(8,128)} %self_ref.1), custom_call_target="tpu_custom_call" | custom-call | tf_op jit(solution)/shard_map/green/pallas_call | solution.py:299
  9.8 27.3 %exchange.1 = (f32[16,2,40,40]{3,2,1,0:T(8,128)}, f32[1,128]{1,0:T(1,128)}) custom-call(s32[1]{0:T(128)S(6)} %copy.12.mult_ref, s32[1,16]{1,0:T(1,128)} %bitcast.3, f32[128,128]{1,0:T(8,128)} %get-tuple-element.4.density_ref, f32[16,40,128]{2,1,0:T(8,128)} %get-tuple-element.5.local_ref, f32[40,40]{1,0:T(8,128)} %rotation_ref.1, f32[4096,128]{1,0:T(8,128)} %bitcast.2), custom_call_target="tpu_custom_call" | custom-call | tf_op jit(solution)/shard_map/exchange/pallas_call | solution.py:314
  37.1 2.0 %copy.13 = f32[16,2,40,40]{3,2,1,0:T(8,128)} copy(f32[16,2,40,40]{3,2,1,0:T(8,128)} %get-tuple-element.8) | data formatting | bytes 409600
  39.1 1.2 %copy.14 = f32[1,128]{1,0:T(1,128)} copy(f32[1,128]{1,0:T(1,128)} %get-tuple-element.9) | data formatting | bytes 1024
where the time goes:
time: 40.5 us; the launch traced here: 40.2 us
  Pallas kernels  34.3 us (85%)
  local copies, waits for them, and re-layouts  4.65 us (11%)
  between operations  1.29 us (3%)
    pallas_call x1, Pallas kernels, local(): pl.pallas_call(functools.partial(exchange_kernel, ka_count, freq_count),...  27.3 us
    pallas_call x1, Pallas kernels, local(): pl.pallas_call(functools.partial(green_kernel, thermal), out_shape=(jax.S...  6.98 us
    unnamed x3, local copies, waits for them, and re-layouts  4.65 us

commit v1 on v0

v1 whole, which is shorter than its diff:
```python
import functools
import math

import jax
import jax.numpy as jnp
from jax import lax
from jax.experimental import pallas as pl
from jax.experimental.pallas import tpu as pltpu
from jax.sharding import PartitionSpec as P

NS_STEPS = 3
PARTS = 2
HALF = 64
F32 = jnp.float32
BF16 = jnp.bfloat16
MESH = pl.DeviceIdType.MESH


def split(value):
    high = value.astype(BF16)
    return high, (value - high.astype(F32)).astype(BF16)


def dot3(first, second):
    one = functools.partial(jnp.dot, preferred_element_type=F32)
    return one(first[0], second[0]) + (one(first[1], second[0]) + one(first[0], second[1]))


def exact_dot(first, second):
    return jnp.dot(first, second, precision=lax.Precision.HIGHEST, preferred_element_type=F32)


def lanes(shape):
    return lax.broadcasted_iota(jnp.int32, shape, len(shape) - 1)


def rows(shape):
    return lax.broadcasted_iota(jnp.int32, shape, 0)


def swap(pair):
    turned = pltpu.roll(pair, HALF, 1)
    return jnp.where(lanes(pair.shape) < HALF, -turned, turned)


def tall(top, bottom):
    gap = jnp.zeros((HALF - top.shape[0], top.shape[1]), F32)
    return jnp.concatenate([top, gap, bottom, gap], axis=0)


def packed(real, imag):
    gap = jnp.zeros((real.shape[0], HALF - real.shape[1]), F32)
    return jnp.concatenate([real, gap, imag, gap], axis=1)


def charge_form(density):
    square = density.shape
    row, lane = rows(square), lanes(square)
    upper = jnp.where(row < lane, 2.0 * density, jnp.where(row == lane, density, 0.0))
    lower = jnp.where(row > lane, 2.0 * density, 0.0)
    cross = lower - jnp.transpose(lower)
    first = jnp.concatenate([upper, jnp.zeros(square, F32)], axis=1)
    return jnp.concatenate([first, jnp.concatenate([cross, upper], axis=1)], axis=0)


def cycle_kernel(
    ka_count, freq_count, thermal,
    mult_ref, owner_ref, energy_ref, proj_ref, self_ref, rotation_ref, orbital_ref,
    green_ref, slab_ref,
    columns, high, low, density_out, density_in, sums, half_in, half, chip_in, gathered,
    rates, charge_out, charge_in,
    orbital_sem, density_sem, half_sem, chip_sem, gather_sem, forward_sem, charge_sem,
):
    me, freq_me = lax.axis_index("ka"), lax.axis_index("freq")
    core, chip = lax.rem(me, 2), me // 2
    partner = me + 1 - 2 * core
    slots, orbs = self_ref.shape[0], self_ref.shape[2]
    bands = energy_ref.shape[1]
    slabs = columns.shape[0] // (2 * bands)
    owner_chips, _, each, _, wide = sums.shape
    chips = ka_count // 2
    full = owner_chips == chips
    weight = mult_ref[0].astype(F32)

    def when_owner(index, action):
        if full:
            action()
        else:
            pl.when(index < owner_chips)(action)

    def owned_chip(index):
        return index if full else jnp.minimum(index, owner_chips - 1)

    def remote(source, target, sems, at, **where):
        return pltpu.make_async_remote_copy(
            src_ref=source, dst_ref=target, send_sem=sems.at[0, at], recv_sem=sems.at[1, at],
            device_id=where, device_id_type=MESH,
        )

    load = pltpu.make_async_copy(orbital_ref, columns, orbital_sem)
    load.start()
    barrier = pltpu.get_barrier_semaphore()
    for j in range(1, ka_count):
        pl.semaphore_signal(barrier, inc=1, device_id={"ka": lax.rem(me + j, ka_count)}, device_id_type=MESH)
    for j in range(1, freq_count):
        pl.semaphore_signal(
            barrier, inc=1, device_id={"freq": lax.rem(freq_me + j, freq_count)}, device_id_type=MESH
        )

    across_re, across_im = proj_ref[0, 0], proj_ref[0, 1]
    pair = jnp.transpose(tall(across_re, across_im))
    swapped = swap(pair)
    weights_pp = split(jnp.concatenate([pair, swapped], axis=0))
    energy = energy_ref[...]
    energy_col = jnp.transpose(jnp.broadcast_to(energy, (bands, bands)))
    lane = lanes((orbs, wide))
    unit = jnp.where(lane == rows((orbs, wide)), 1.0, 0.0).astype(F32)

    def green_part(at):
        omega = [(2 * (q * freq_count + freq_me) + 1).astype(F32) * (math.pi * thermal) for q in at]
        inv = [1.0 / (w * w + energy * energy) for w in omega]
        bare_re = [-energy * v for v in inv]
        bare_im = [-w * v for w, v in zip(omega, inv)]
        c_re = [across_re * r + across_im * i for r, i in zip(bare_re, bare_im)]
        c_im = [across_re * i - across_im * r for r, i in zip(bare_re, bare_im)]
        g = [dot3(split(jnp.concatenate([a, b], axis=1)), weights_pp) for a, b in zip(c_re, c_im)]
        s = [split(packed(self_ref[q, 0], self_ref[q, 1])) for q in at]
        first = [
            split(tall(jnp.concatenate([a, b, c], axis=1), jnp.concatenate([-b, a, swap(c)], axis=1)))
            for a, b, c in zip(c_re, c_im, g)
        ]
        out = [dot3(a, b) for a, b in zip(s, first)]
        sc_re = [o[:, :bands] for o in out]
        sc_im = [o[:, bands : 2 * bands] for o in out]
        a1 = [o[:, 2 * bands :] for o in out]
        real_a = [split(tall(a, swap(a))) for a in a1]
        a2 = [dot3(split(a), r) for a, r in zip(a1, real_a)]
        a3 = [dot3(split(a), r) for a, r in zip(a2, real_a)]
        h = [a + b + c for a, b, c in zip(a1, a2, a3)]
        poly = [unit + a + dot3(split(a), split(tall(b, swap(b)))) for a, b in zip(h, a3)]
        real_sc = [
            split(tall(jnp.concatenate([a, b], axis=1), jnp.concatenate([-b, a], axis=1)))
            for a, b in zip(sc_re, sc_im)
        ]
        poly = [split(p) for p in poly]
        wg = [dot3(p, r) for p, r in zip(poly, real_a)]
        for q, one_g, one_w in zip(at, g, wg):
            one = weight * (one_g + dot3(split(one_g), split(tall(one_w, swap(one_w)))))
            place = (q // (2 * each), (q // each) % 2, q % each)
            sums[place] = jnp.where(lane >= HALF + orbs, weight, one)
        gain = None
        for w, p, r in zip(omega, poly, real_sc):
            one_v = dot3(p, r)
            inv_col = 1.0 / (w * w + energy_col * energy_col)
            left = split(pair * (-energy_col * inv_col) + swapped * (-w * inv_col))
            v_re, v_im = one_v[:, :bands], one_v[:, bands:]
            right = split(tall(one_v, jnp.concatenate([-v_im, v_re], axis=1)))
            term = dot3(left, right)
            gain = term if gain is None else gain + term
        return gain

    part_chips = owner_chips // PARTS
    half_copies, gain = [], None
    for part in range(PARTS):
        per = slots // PARTS
        one = green_part([part * per + g for g in range(per)])
        gain = one if gain is None else gain + one
        if part == 0:
            pl.semaphore_wait(barrier, ka_count + freq_count - 2)
        chunk = pl.ds(part * part_chips, part_chips)
        half_copies.append(remote(sums.at[chunk, 1 - core], half_in.at[chunk], half_sem, part, ka=partner))
        half_copies[-1].start()

    e_re, e_im = gain[:, :bands], gain[:, bands:]
    d_re = thermal * (e_re + jnp.transpose(e_re))
    d_im = thermal * (e_im - jnp.transpose(e_im))
    square = (bands, bands)
    density_out[...] = jnp.where(rows(square) <= lanes(square), d_re, d_im)
    density_copies = []
    for j in range(1, freq_count):
        density_copies.append(
            remote(density_out, density_in.at[j - 1], density_sem, j - 1, freq=lax.rem(freq_me + j, freq_count))
        )
        density_copies[-1].start()

    for part in range(PARTS):
        half_copies[part].wait_recv()
        for c in range(part * part_chips, (part + 1) * part_chips):
            half[c] = sums[c, core] + half_in[c]
    chip_copies = []
    for j in range(1, chips):
        to = lax.rem(chip + j, chips)
        copy = remote(half.at[owned_chip(to)], chip_in.at[j - 1], chip_sem, j - 1, ka=to * 2 + core)
        chip_copies.append((copy, to))
        when_owner(to, copy.start)

    load.wait()
    for s in range(slabs):
        high[s], low[s] = split(columns[pl.ds(s, 2 * bands, stride=slabs), :])

    for copy in density_copies:
        copy.wait()
    density = density_out[...]
    for j in range(1, freq_count):
        density = density + density_in[j - 1]
    form = split(charge_form(density))
    for s in range(slabs):
        product = dot3(form, (high[s], low[s]))
        one = high[s].astype(F32) + low[s].astype(F32)
        rates[pl.ds(s, 1), :] = weight * jnp.sum(product * one, axis=0, keepdims=True)
    selector = jnp.where(owner_ref[...] == rows((slabs, slabs)), 1.0, 0.0).astype(F32)
    owned = exact_dot(selector, rates[...])
    for d in range(slabs):
        charge_out[d, 0:1, :] = owned[d : d + 1]
        charge_out[d, 1:2, :] = jnp.full((1, owned.shape[1]), weight, F32)
    charge_copies = []
    for j in range(1, ka_count):
        to = lax.rem(me + j, ka_count)
        charge_copies.append(remote(charge_out.at[to], charge_in.at[j - 1], charge_sem, j - 1, ka=to))
        charge_copies[-1].start()

    spot = owned_chip(chip)
    gather_copies = [
        remote(
            gathered.at[spot, core], gathered.at[spot, core], gather_sem, j - 1,
            ka=lax.rem(chip + j, chips) * 2 + core,
        )
        for j in range(1, chips)
    ]
    sources = [chip] + [lax.rem(chip + chips - j, chips) for j in range(1, chips)]
    forward_copies = [
        remote(
            gathered.at[owned_chip(source), core], gathered.at[owned_chip(source), core],
            forward_sem, j, ka=partner,
        )
        for j, source in enumerate(sources)
    ]

    def reduce_and_send():
        for copy, _ in chip_copies:
            copy.wait_recv()
        turn = rotation_ref[...]
        gap = jnp.zeros((orbs, HALF - orbs), F32)
        zero = jnp.zeros((orbs, HALF), F32)
        right = tall(jnp.concatenate([turn, gap, zero], axis=1), jnp.concatenate([zero, turn, gap], axis=1))
        left = jnp.transpose(turn)
        for e in range(each):
            acc = half[spot, e]
            for j in range(1, chips):
                acc = acc + chip_in[j - 1, e]
            share = acc / acc[:1, wide - 1 :]
            gathered[spot, core, e] = exact_dot(left, exact_dot(share, right))
        for copy in gather_copies:
            copy.start()
        forward_copies[0].start()

    when_owner(chip, reduce_and_send)
    for j in range(1, chips):

        def pass_on(j=j):
            gather_copies[j - 1].wait_recv()
            forward_copies[j].start()

        when_owner(sources[j], pass_on)
    for copy in charge_copies:
        copy.wait()
    acc = charge_out[me]
    for j in range(1, ka_count):
        acc = acc + charge_in[j - 1]
    slab_ref[...] = acc[0:1] / acc[1:2]
    for j in range(chips):
        when_owner(sources[j], forward_copies[j].wait)
    green_ref[...] = gathered[...]
    for copy in half_copies:
        copy.wait_send()
    for copy, to in chip_copies:
        when_owner(to, copy.wait_send)

    def sent():
        for copy in gather_copies:
            copy.wait_send()

    when_owner(chip, sent)


def finish_kernel(gathered_ref, slab_in_ref, green_ref, slab_ref):
    orbs = green_ref.shape[3]
    each = gathered_ref.shape[2]
    for q in range(green_ref.shape[0]):
        value = gathered_ref[q // (2 * each), (q // each) % 2, q % each]
        green_ref[q, 0] = value[:, :orbs]
        green_ref[q, 1] = pltpu.roll(value, HALF, 1)[:, :orbs]
    slab_ref[...] = slab_in_ref[...]


def local(energy, projector, self_energy, multiplicity, orbitals, owner, rotation):
    slots, orbs = self_energy.shape[0], self_energy.shape[2]
    bands = energy.shape[1]
    slab_count, point_count = orbitals.shape[3], orbitals.shape[4]
    freq_count, ka_count = lax.axis_size("freq"), lax.axis_size("ka")
    thermal = 0.25 / (slots * freq_count)
    vmem = pl.BlockSpec(memory_space=pltpu.VMEM)
    smem = pl.BlockSpec(memory_space=pltpu.SMEM)
    owner_chips = min(slots, ka_count) // 2
    each = slots // (2 * owner_chips)
    chips, others = ka_count // 2, max(freq_count - 1, 1)
    tile = (each, orbs, 2 * HALF)
    dma = pltpu.SemaphoreType.DMA
    columns = orbitals.reshape(2 * bands * slab_count, point_count)
    gathered, slab = pl.pallas_call(
        functools.partial(cycle_kernel, ka_count, freq_count, thermal),
        out_shape=(
            jax.ShapeDtypeStruct((owner_chips, 2) + tile, F32),
            jax.ShapeDtypeStruct((1, point_count), F32),
        ),
        in_specs=[smem, vmem, vmem, vmem, vmem, vmem, pl.BlockSpec(memory_space=pl.ANY)],
        out_specs=(vmem, vmem),
        scratch_shapes=[
            pltpu.VMEM(columns.shape, F32),
            pltpu.VMEM((slab_count, 2 * bands, point_count), BF16),
            pltpu.VMEM((slab_count, 2 * bands, point_count), BF16),
            pltpu.VMEM((bands, bands), F32),
            pltpu.VMEM((others, bands, bands), F32),
            pltpu.VMEM((owner_chips, 2) + tile, F32),
            pltpu.VMEM((owner_chips,) + tile, F32),
            pltpu.VMEM((owner_chips,) + tile, F32),
            pltpu.VMEM((chips - 1,) + tile, F32),
            pltpu.VMEM((owner_chips, 2) + tile, F32),
            pltpu.VMEM((slab_count, point_count), F32),
            pltpu.VMEM((slab_count, 2, point_count), F32),
            pltpu.VMEM((ka_count - 1, 2, point_count), F32),
            dma,
            dma((2, others)),
            dma((2, PARTS)),
            dma((2, chips - 1)),
            dma((2, chips - 1)),
            dma((2, chips)),
            dma((2, ka_count - 1)),
        ],
        compiler_params=pltpu.CompilerParams(collective_id=0, has_side_effects=True),
        name="cycle",
    )(
        multiplicity, owner.reshape(1, slab_count), energy, jnp.swapaxes(projector, 2, 3),
        self_energy, rotation, columns,
    )
    return pl.pallas_call(
        finish_kernel,
        out_shape=(
            jax.ShapeDtypeStruct((slots, 2, orbs, orbs), F32),
            jax.ShapeDtypeStruct((1, point_count), F32),
        ),
        in_specs=[vmem, vmem],
        out_specs=(vmem, vmem),
        name="finish",
    )(gathered, slab)


def solution(mesh):
    in_specs = (
        P("ka", None),
        P("ka", None, None, None),
        P("freq", None, None, None),
        P("ka"),
        P("ka", None, None, None, "freq"),
        P(),
        P(),
    )
    out_specs = (P("freq", None, None, None), P("ka", "freq"))
    return jax.shard_map(local, mesh=mesh, in_specs=in_specs, out_specs=out_specs, check_vma=False)
```

time: 40.5 us -> 27.9 us (0.69)
  Pallas kernels: 34.3 us -> 26.4 us
  local copies, waits for them, and re-layouts: 4.65 us -> 0 us
    pallas_call x2, Pallas kernels: 34.3 us -> 26.4 us  [the longest x1 24.4 us: local(): pl.pallas_call(functools.partial(cycle_kernel, ka_count, freq_count, ther...]
    unnamed x3 -> x0, local copies, waits for them, and re-layouts: 4.65 us -> none
where the time goes in v1:
time: 27.9 us; the launch traced here: 27.7 us
  Pallas kernels  26.4 us (95%)
  between operations  1.29 us (5%)
    pallas_call x1, Pallas kernels, local(): pl.pallas_call(functools.partial(cycle_kernel, ka_count, freq_count, ther...  24.4 us
    pallas_call x1, Pallas kernels, local(): pl.pallas_call(finish_kernel, out_shape=(jax.ShapeDtypeStruct((slots, 2,...  1.97 us

profile of v1, /device:TPU:0, one launch (start us, length us, event | category | flops | bytes accessed | tf_op | source)
XLA Modules:
  0.0 27.7 jit_solution(13885887336325032833)
XLA Ops:
  1.3 24.4 %cycle.1 = (f32[8,2,1,40,128]{4,3,2,1,0:T(8,128)}, f32[1,128]{1,0:T(1,128)}) custom-call(s32[1]{0:T(128)S(6)} %copy.9.mult_ref, s32[1,16]{1,0:T(1,128)} %bitcast.5, f32[1,128]{1,0:T(1,128)} %energy_ref.1, f32[1,2,40,128]{3,2,1,0:T(8,128)} %bitcast.4, f32[16,2,40,40]{3,2,1,0:T(8,128)} %self_ref.1, f32[40,40]{1,0:T(8,128)} %rotation_ref.1, f32[4096,128]{1,0:T(8,128)} %bitcast.3), custom_call_target="tpu_custom_call" | custom-call | tf_op jit(solution)/shard_map/cycle/pallas_call | solution.py:310
  25.7 2.0 %finish.1 = (f32[16,2,40,40]{3,2,1,0:T(8,128)}, f32[1,128]{1,0:T(1,128)}) custom-call(f32[8,2,1,40,128]{4,3,2,1,0:T(8,128)} %get-tuple-element.4.gathered_ref, f32[1,128]{1,0:T(1,128)} %get-tuple-element.5.slab_in_ref), custom_call_target="tpu_custom_call" | custom-call | tf_op jit(solution)/shard_map/finish/pallas_call | solution.py:346

commit v2 on v1

--- a/solution.py
+++ b/solution.py
@@ -10,6 +10,7 @@
 
 NS_STEPS = 3
 PARTS = 2
+EARLY = 4
 HALF = 64
 F32 = jnp.float32
 BF16 = jnp.bfloat16
@@ -24,10 +25,6 @@
 def dot3(first, second):
     one = functools.partial(jnp.dot, preferred_element_type=F32)
     return one(first[0], second[0]) + (one(first[1], second[0]) + one(first[0], second[1]))
-
-
-def exact_dot(first, second):
-    return jnp.dot(first, second, precision=lax.Precision.HIGHEST, preferred_element_type=F32)
 
 
 def lanes(shape):
@@ -65,18 +62,18 @@
 
 def cycle_kernel(
     ka_count, freq_count, thermal,
-    mult_ref, owner_ref, energy_ref, proj_ref, self_ref, rotation_ref, orbital_ref,
+    mult_ref, owner_ref, energy_ref, proj_ref, self_hbm, rotation_ref, orbital_ref,
     green_ref, slab_ref,
-    columns, high, low, density_out, density_in, sums, half_in, half, chip_in, gathered,
+    self_ref, columns, high, low, coupled, series, density_out, density_in, sums, half_in, half, chip_in, gathered,
     rates, charge_out, charge_in,
-    orbital_sem, density_sem, half_sem, chip_sem, gather_sem, forward_sem, charge_sem,
+    self_sem, orbital_sem, density_sem, half_sem, chip_sem, gather_sem, forward_sem, charge_sem,
 ):
     me, freq_me = lax.axis_index("ka"), lax.axis_index("freq")
     core, chip = lax.rem(me, 2), me // 2
     partner = me + 1 - 2 * core
     slots, orbs = self_ref.shape[0], self_ref.shape[2]
     bands = energy_ref.shape[1]
-    slabs = columns.shape[0] // (2 * bands)
+    slabs, points = columns.shape[0] // (2 * bands), columns.shape[1]
     owner_chips, _, each, _, wide = sums.shape
     chips = ka_count // 2
     full = owner_chips == chips
@@ -97,6 +94,8 @@
             device_id=where, device_id_type=MESH,
         )
 
+    fetch = pltpu.make_async_copy(self_hbm, self_ref, self_sem)
+    fetch.start()
     load = pltpu.make_async_copy(orbital_ref, columns, orbital_sem)
     load.start()
     barrier = pltpu.get_barrier_semaphore()
@@ -116,8 +115,15 @@
     lane = lanes((orbs, wide))
     unit = jnp.where(lane == rows((orbs, wide)), 1.0, 0.0).astype(F32)
 
+    def omega_of(q):
+        return (2 * (q * freq_count + freq_me) + 1).astype(F32) * (math.pi * thermal)
+
+    def real_wide(value):
+        re, im = value[:, :bands], value[:, bands:]
+        return split(tall(value, jnp.concatenate([-im, re], axis=1)))
+
     def green_part(at):
-        omega = [(2 * (q * freq_count + freq_me) + 1).astype(F32) * (math.pi * thermal) for q in at]
+        omega = [omega_of(q) for q in at]
         inv = [1.0 / (w * w + energy * energy) for w in omega]
         bare_re = [-energy * v for v in inv]
         bare_im = [-w * v for w, v in zip(omega, inv)]
@@ -130,47 +136,61 @@
             for a, b, c in zip(c_re, c_im, g)
         ]
         out = [dot3(a, b) for a, b in zip(s, first)]
-        sc_re = [o[:, :bands] for o in out]
-        sc_im = [o[:, bands : 2 * bands] for o in out]
         a1 = [o[:, 2 * bands :] for o in out]
         real_a = [split(tall(a, swap(a))) for a in a1]
         a2 = [dot3(split(a), r) for a, r in zip(a1, real_a)]
         a3 = [dot3(split(a), r) for a, r in zip(a2, real_a)]
         h = [a + b + c for a, b, c in zip(a1, a2, a3)]
         poly = [unit + a + dot3(split(a), split(tall(b, swap(b)))) for a, b in zip(h, a3)]
-        real_sc = [
-            split(tall(jnp.concatenate([a, b], axis=1), jnp.concatenate([-b, a], axis=1)))
-            for a, b in zip(sc_re, sc_im)
-        ]
+        for q, o, p in zip(at, out, poly):
+            coupled[q], series[q] = o[:, : 2 * bands], p
         poly = [split(p) for p in poly]
         wg = [dot3(p, r) for p, r in zip(poly, real_a)]
         for q, one_g, one_w in zip(at, g, wg):
             one = weight * (one_g + dot3(split(one_g), split(tall(one_w, swap(one_w)))))
             place = (q // (2 * each), (q // each) % 2, q % each)
             sums[place] = jnp.where(lane >= HALF + orbs, weight, one)
+
+    def density_part(at):
         gain = None
-        for w, p, r in zip(omega, poly, real_sc):
-            one_v = dot3(p, r)
+        for q in at:
+            w = omega_of(q)
+            one_v = dot3(split(series[q]), real_wide(coupled[q]))
             inv_col = 1.0 / (w * w + energy_col * energy_col)
             left = split(pair * (-energy_col * inv_col) + swapped * (-w * inv_col))
-            v_re, v_im = one_v[:, :bands], one_v[:, bands:]
-            right = split(tall(one_v, jnp.concatenate([-v_im, v_re], axis=1)))
-            term = dot3(left, right)
+            term = dot3(left, real_wide(one_v))
             gain = term if gain is None else gain + term
         return gain
 
     part_chips = owner_chips // PARTS
-    half_copies, gain = [], None
+    half_copies, gain = [], 0.0
+    per = slots // PARTS
+    fetch.wait()
     for part in range(PARTS):
-        per = slots // PARTS
-        one = green_part([part * per + g for g in range(per)])
-        gain = one if gain is None else gain + one
+        green_part([part * per + g for g in range(per)])
+        if part > 0:
+            gain = gain + density_part(range((part - 1) * per, part * per))
         if part == 0:
             pl.semaphore_wait(barrier, ka_count + freq_count - 2)
         chunk = pl.ds(part * part_chips, part_chips)
         half_copies.append(remote(sums.at[chunk, 1 - core], half_in.at[chunk], half_sem, part, ka=partner))
         half_copies[-1].start()
 
+    chip_copies = []
+    for part in range(PARTS):
+        half_copies[part].wait_recv()
+        for c in range(part * part_chips, (part + 1) * part_chips):
+            half[c] = sums[c, core] + half_in[c]
+        for j in range(1, chips):
+            to = lax.rem(chip + j, chips)
+            copy = remote(half.at[owned_chip(to)], chip_in.at[j - 1], chip_sem, j - 1, ka=to * 2 + core)
+            if part == 0:
+                chip_copies.append((copy, to))
+            inside = jnp.logical_and(to >= part * part_chips, to < (part + 1) * part_chips)
+            pl.when(inside)(copy.start)
+        if part == PARTS - 2:
+            gain = gain + density_part(range(slots - per, slots - per + per // EARLY))
+    gain = gain + density_part(range(slots - per + per // EARLY, slots))
     e_re, e_im = gain[:, :bands], gain[:, bands:]
     d_re = thermal * (e_re + jnp.transpose(e_re))
     d_im = thermal * (e_im - jnp.transpose(e_im))
@@ -183,33 +203,63 @@
         )
         density_copies[-1].start()
 
-    for part in range(PARTS):
-        half_copies[part].wait_recv()
-        for c in range(part * part_chips, (part + 1) * part_chips):
-            half[c] = sums[c, core] + half_in[c]
-    chip_copies = []
-    for j in range(1, chips):
-        to = lax.rem(chip + j, chips)
-        copy = remote(half.at[owned_chip(to)], chip_in.at[j - 1], chip_sem, j - 1, ka=to * 2 + core)
-        chip_copies.append((copy, to))
-        when_owner(to, copy.start)
-
     load.wait()
     for s in range(slabs):
-        high[s], low[s] = split(columns[pl.ds(s, 2 * bands, stride=slabs), :])
-
+        place = pl.ds((s % 2) * points, points)
+        high[s // 2, :, place], low[s // 2, :, place] = split(columns[pl.ds(s, 2 * bands, stride=slabs), :])
+
+    spot = owned_chip(chip)
+    gather_copies = [
+        remote(
+            gathered.at[spot, core], gathered.at[spot, core], gather_sem, j - 1,
+            ka=lax.rem(chip + j, chips) * 2 + core,
+        )
+        for j in range(1, chips)
+    ]
+    sources = [chip] + [lax.rem(chip + chips - j, chips) for j in range(1, chips)]
+    forward_copies = [
+        remote(
+            gathered.at[owned_chip(source), core], gathered.at[owned_chip(source), core],
+            forward_sem, j, ka=partner,
+        )
+        for j, source in enumerate(sources)
+    ]
+
+    def reduce_and_send():
+        for copy, _ in chip_copies:
+            copy.wait_recv()
+        turn = rotation_ref[...]
+        gap = jnp.zeros((orbs, HALF - orbs), F32)
+        zero = jnp.zeros((orbs, HALF), F32)
+        right = tall(jnp.concatenate([turn, gap, zero], axis=1), jnp.concatenate([zero, turn, gap], axis=1))
+        left = split(jnp.transpose(turn))
+        right = split(right)
+        for e in range(each):
+            acc = half[spot, e]
+            for j in range(1, chips):
+                acc = acc + chip_in[j - 1, e]
+            share = acc / acc[:1, wide - 1 :]
+            gathered[spot, core, e] = dot3(left, split(dot3(split(share), right)))
+        for copy in gather_copies:
+            copy.start()
+        forward_copies[0].start()
+
+    when_owner(chip, reduce_and_send)
     for copy in density_copies:
         copy.wait()
     density = density_out[...]
     for j in range(1, freq_count):
         density = density + density_in[j - 1]
     form = split(charge_form(density))
-    for s in range(slabs):
-        product = dot3(form, (high[s], low[s]))
-        one = high[s].astype(F32) + low[s].astype(F32)
-        rates[pl.ds(s, 1), :] = weight * jnp.sum(product * one, axis=0, keepdims=True)
+    for s in range(slabs // 2):
+        one = (high[s], low[s])
+        product = dot3(form, one) * (one[0].astype(F32) + one[1].astype(F32))
+        rate = weight * jnp.sum(product, axis=0, keepdims=True)
+        rates[pl.ds(2 * s, 1), :], rates[pl.ds(2 * s + 1, 1), :] = rate[:, :points], rate[:, points:]
     selector = jnp.where(owner_ref[...] == rows((slabs, slabs)), 1.0, 0.0).astype(F32)
-    owned = exact_dot(selector, rates[...])
+    parted = split(rates[...])
+    owned = jnp.dot(selector.astype(BF16), parted[0], preferred_element_type=F32)
+    owned = owned + jnp.dot(selector.astype(BF16), parted[1], preferred_element_type=F32)
     for d in range(slabs):
         charge_out[d, 0:1, :] = owned[d : d + 1]
         charge_out[d, 1:2, :] = jnp.full((1, owned.shape[1]), weight, F32)
@@ -219,42 +269,6 @@
         charge_copies.append(remote(charge_out.at[to], charge_in.at[j - 1], charge_sem, j - 1, ka=to))
         charge_copies[-1].start()
 
-    spot = owned_chip(chip)
-    gather_copies = [
-        remote(
-            gathered.at[spot, core], gathered.at[spot, core], gather_sem, j - 1,
-            ka=lax.rem(chip + j, chips) * 2 + core,
-        )
-        for j in range(1, chips)
-    ]
-    sources = [chip] + [lax.rem(chip + chips - j, chips) for j in range(1, chips)]
-    forward_copies = [
-        remote(
-            gathered.at[owned_chip(source), core], gathered.at[owned_chip(source), core],
-            forward_sem, j, ka=partner,
-        )
-        for j, source in enumerate(sources)
-    ]
-
-    def reduce_and_send():
-        for copy, _ in chip_copies:
-            copy.wait_recv()
-        turn = rotation_ref[...]
-        gap = jnp.zeros((orbs, HALF - orbs), F32)
-        zero = jnp.zeros((orbs, HALF), F32)
-        right = tall(jnp.concatenate([turn, gap, zero], axis=1), jnp.concatenate([zero, turn, gap], axis=1))
-        left = jnp.transpose(turn)
-        for e in range(each):
-            acc = half[spot, e]
-            for j in range(1, chips):
-                acc = acc + chip_in[j - 1, e]
-            share = acc / acc[:1, wide - 1 :]
-            gathered[spot, core, e] = exact_dot(left, exact_dot(share, right))
-        for copy in gather_copies:
-            copy.start()
-        forward_copies[0].start()
-
-    when_owner(chip, reduce_and_send)
     for j in range(1, chips):
 
         def pass_on(j=j):
@@ -301,6 +315,7 @@
     thermal = 0.25 / (slots * freq_count)
     vmem = pl.BlockSpec(memory_space=pltpu.VMEM)
     smem = pl.BlockSpec(memory_space=pltpu.SMEM)
+    hbm = pl.BlockSpec(memory_space=pl.ANY)
     owner_chips = min(slots, ka_count) // 2
     each = slots // (2 * owner_chips)
     chips, others = ka_count // 2, max(freq_count - 1, 1)
@@ -313,12 +328,15 @@
             jax.ShapeDtypeStruct((owner_chips, 2) + tile, F32),
             jax.ShapeDtypeStruct((1, point_count), F32),
         ),
-        in_specs=[smem, vmem, vmem, vmem, vmem, vmem, pl.BlockSpec(memory_space=pl.ANY)],
+        in_specs=[smem, vmem, vmem, vmem, hbm, vmem, hbm],
         out_specs=(vmem, vmem),
         scratch_shapes=[
+            pltpu.VMEM(self_energy.shape, F32),
             pltpu.VMEM(columns.shape, F32),
-            pltpu.VMEM((slab_count, 2 * bands, point_count), BF16),
-            pltpu.VMEM((slab_count, 2 * bands, point_count), BF16),
+            pltpu.VMEM((slab_count // 2, 2 * bands, 2 * point_count), BF16),
+            pltpu.VMEM((slab_count // 2, 2 * bands, 2 * point_count), BF16),
+            pltpu.VMEM((slots, orbs, 2 * bands), F32),
+            pltpu.VMEM((slots, orbs, 2 * HALF), F32),
             pltpu.VMEM((bands, bands), F32),
             pltpu.VMEM((others, bands, bands), F32),
             pltpu.VMEM((owner_chips, 2) + tile, F32),
@@ -329,6 +347,7 @@
             pltpu.VMEM((slab_count, point_count), F32),
             pltpu.VMEM((slab_count, 2, point_count), F32),
             pltpu.VMEM((ka_count - 1, 2, point_count), F32),
+            dma,
             dma,
             dma((2, others)),
             dma((2, PARTS)),

time: 27.9 us -> 27.6 us (0.989)
  Pallas kernels: 26.4 us -> 26.1 us
    pallas_call x1, Pallas kernels: 24.4 us -> 24.1 us  [local(): pl.pallas_call(functools.partial(cycle_kernel, ka_count, freq_count, ther...]
where the time goes in v2:
time: 27.6 us; the launch traced here: 27.4 us
  Pallas kernels  26.1 us (95%)
  between operations  1.29 us (5%)
    pallas_call x1, Pallas kernels, local(): pl.pallas_call(functools.partial(cycle_kernel, ka_count, freq_count, ther...  24.1 us
    pallas_call x1, Pallas kernels, local(): pl.pallas_call(finish_kernel, out_shape=(jax.ShapeDtypeStruct((slots, 2,...  1.97 us

profile of v2, /device:TPU:0, one launch (start us, length us, event | category | flops | bytes accessed | tf_op | source)
XLA Modules:
  0.0 27.4 jit_solution(4604916831224375682)
XLA Ops:
  1.3 24.1 %cycle.1 = (f32[8,2,1,40,128]{4,3,2,1,0:T(8,128)}, f32[1,128]{1,0:T(1,128)}) custom-call(s32[1]{0:T(128)S(6)} %copy.9.mult_ref, s32[1,16]{1,0:T(1,128)} %bitcast.5, f32[1,128]{1,0:T(1,128)} %energy_ref.1, f32[1,2,40,128]{3,2,1,0:T(8,128)} %bitcast.4, f32[16,2,40,40]{3,2,1,0:T(8,128)} %self_hbm.1, f32[40,40]{1,0:T(8,128)} %rotation_ref.1, f32[4096,128]{1,0:T(8,128)} %bitcast.3), custom_call_target="tpu_custom_call" | custom-call | tf_op jit(solution)/shard_map/cycle/pallas_call | solution.py:325
  25.4 2.0 %finish.1 = (f32[16,2,40,40]{3,2,1,0:T(8,128)}, f32[1,128]{1,0:T(1,128)}) custom-call(f32[8,2,1,40,128]{4,3,2,1,0:T(8,128)} %get-tuple-element.4.gathered_ref, f32[1,128]{1,0:T(1,128)} %get-tuple-element.5.slab_in_ref), custom_call_target="tpu_custom_call" | custom-call | tf_op jit(solution)/shard_map/finish/pallas_call | solution.py:365
